TPU v7x, 32 devices: a whole 2x2x4 slice. The times are simulated.
32 devices in a mesh: gx: 8 (over z, core), gy: 4 (over y, x).
Axes of the slice: x: 2, y: 2, z: 4, core: 2. Of those that a mesh axis runs over, the one named last changes fastest.
Arguments:
- coarse: bfloat16 [32, 8, 64, 128], P(None, None, 'gy'), may hold values from -6 to 6
- w_three: bfloat16 [27, 16, 32], replicated, may hold values from -0.5 to 0.5
- w_four: bfloat16 [27, 16], replicated, may hold values from -0.75 to 0.75
- elec_field: bfloat16 [3, 32, 256, 512], P(None, 'gx', 'gy'), may hold values from -6 to 6
- temp_grad: bfloat16 [3, 32, 256, 512], P(None, 'gx', 'gy'), may hold values from -6 to 6
- adjoint: bfloat16 [32, 256, 512], P('gx', 'gy'), may hold values from -6 to 6
- adjoint_grad: bfloat16 [3, 32, 256, 512], P(None, 'gx', 'gy'), may hold values from -6 to 6
Outputs:
- density: float32 [32, 256, 512], P('gx', 'gy')
- grad_three: float32 [27, 16, 32], replicated
- grad_four: float32 [27, 16], replicated
All inputs are finite; a program needn't handle non-finite values.
Results may differ from a plain program's by a relative error of at most 0.0053.
Values may be sent and summed in bfloat16 or wider, within the bound.
No kernel may reach another device: no remote copies, remote signals or barrier semaphores. Data moves between devices by JAX's collectives and lax.ppermute only.
A program may use at most 128 MiB of HBM per device.

v0:
```python
import math
import jax
import jax.numpy as jnp
import numpy as np
from jax import lax
from jax.sharding import PartitionSpec as P

HIGH = lax.Precision.HIGHEST


def passed_along(value, axis, by):
    size = lax.axis_size(axis)
    pairs = [(i, i + by) for i in range(size) if 0 <= i + by < size]
    return lax.ppermute(value, axis, pairs)


def tap_tables():
    onehot = np.zeros((8, 8, 27), np.float32)
    strides = (9, 3, 1)
    for offset in range(8):
        for parity in range(8):
            kernel = 0
            usable = True
            for axis_pos in range(3):
                bit_off = offset >> 2 - axis_pos & 1
                bit_par = parity >> 2 - axis_pos & 1
                if bit_off > bit_par:
                    usable = False
                if bit_par == 0:
                    along = 1
                elif bit_off == 0:
                    along = 2
                else:
                    along = 0
                kernel = kernel + along * strides[axis_pos]
            if usable:
                onehot[offset, parity, kernel] = 1.0
    return onehot


def residue_table():
    per_axis = ({0: 1}, {0: 2, 1: 0}, {1: 1}, {1: 2, 2: 0})
    lookup = np.zeros((64, 27, 27), np.float32)
    for residue in range(64):
        res_x, res_y, res_z = (residue // 16, residue // 4 % 4, residue % 4)
        for src_x, tap_x in per_axis[res_x].items():
            for src_y, tap_y in per_axis[res_y].items():
                for src_z, tap_z in per_axis[res_z].items():
                    lookup[
                        residue, 9 * src_x + 3 * src_y + src_z, 9 * tap_x + 3 * tap_y + tap_z
                    ] = 1.0
    return lookup


def bits_of(offset):
    return (offset >> 2 & 1, offset >> 1 & 1, offset & 1)


def shift_last(block):
    return jnp.concatenate([block[..., 1:], jnp.zeros_like(block[..., :1])], -1)


def delay_last(block):
    return jnp.concatenate([jnp.zeros_like(block[..., :1]), block[..., :-1]], -1)


def beside_y(block, steps_by):
    return passed_along(block, "gy", steps_by)


def silu_slope(values):
    sigma_pre = jax.nn.sigmoid(values)
    return sigma_pre * (1.0 + values * (1.0 - sigma_pre))


def coarse_windows(ext_three, count_a, count_b):
    stacked = []
    for offset in range(8):
        bit_a, bit_b, bit_c = bits_of(offset)
        window = ext_three[:, bit_a : bit_a + count_a, bit_b : bit_b + count_b, :]
        if bit_c == 1:
            window = shift_last(window)
        stacked.append(window)
    merged = jnp.stack(stacked)
    return merged.reshape((merged.shape[0] * merged.shape[1],) + merged.shape[2:])


def layer_three_matrix(weight):
    lookup = jnp.asarray(tap_tables(), jnp.bfloat16)
    spread = jnp.einsum("spk,koc->posc", lookup, weight, preferred_element_type=jnp.float32).astype(
        jnp.bfloat16
    )
    return spread.reshape(8 * weight.shape[1], 8 * weight.shape[2])


def layer_four_matrix(w_four):
    lookup = jnp.asarray(residue_table(), jnp.bfloat16)
    spread = jnp.einsum("usk,ki->usi", lookup, w_four, preferred_element_type=jnp.float32).astype(
        jnp.bfloat16
    )
    return spread.reshape(64, 27 * w_four.shape[1])


def hidden_windows(hidden):
    even_x = hidden[0]
    rim_plane = passed_along(even_x, "gx", -1)
    next_x = jnp.concatenate([even_x[:, :, :, 1:], rim_plane], 3)
    along_x = jnp.stack([even_x, hidden[1], next_x])
    even_y = along_x[:, 0]
    rim_side = beside_y(even_y[:, :, :, :, :1], -1)
    next_y = jnp.concatenate([even_y[:, :, :, :, 1:], rim_side], 4)
    along_y = jnp.stack([even_y, along_x[:, 1], next_y], 1)
    even_z = along_y[:, :, 0]
    along_z = jnp.stack([even_z, along_y[:, :, 1], shift_last(even_z)], 2)
    shape = along_z.shape
    return along_z.reshape((27 * shape[3],) + shape[4:])


def gather_back(spread):
    fold_z = jnp.stack([spread[:, :, 0] + delay_last(spread[:, :, 2]), spread[:, :, 1]], 2)
    later_y = fold_z[:, 2]
    rim_side = passed_along(later_y[:, :, :, :, -1:], "gy", 1)
    moved_y = jnp.concatenate([rim_side, later_y[:, :, :, :, :-1]], 4)
    fold_y = jnp.stack([fold_z[:, 0] + moved_y, fold_z[:, 1]], 1)
    later_x = fold_y[2]
    rim_plane = passed_along(later_x, "gx", 1)
    moved_x = jnp.concatenate([rim_plane, later_x[:, :, :, :-1]], 3)
    fold_x = jnp.stack([fold_y[0] + moved_x, fold_y[1]])
    return fold_x.reshape((8,) + fold_x.shape[3:])


def to_storage(classes, count_a, count_b):
    depth = classes.shape[-1]
    split = classes.reshape(4, 4, 4, count_a, count_b, depth).transpose(3, 0, 4, 1, 2, 5)
    return split.reshape(4 * count_a, 4 * count_b, 4 * depth)


def to_classes(fine, count_a, count_b):
    depth = fine.shape[-1] // 4
    split = fine.reshape(count_a, 4, count_b, 4, 4, depth).transpose(1, 3, 4, 0, 2, 5)
    return split.reshape(64, count_a, count_b, depth)


def first_layer(windows_three, weight):
    matrix_three = layer_three_matrix(weight)
    pre_three = jnp.einsum(
        "qk,kabd->qabd", matrix_three, windows_three, preferred_element_type=jnp.float32
    )
    return pre_three.reshape((8, weight.shape[1]) + pre_three.shape[1:])


def three_gradient(g_pre, windows_three):
    chan_out = g_pre.shape[1]
    flat = g_pre.reshape((8 * chan_out,) + g_pre.shape[2:])
    terms = jnp.einsum("qabd,kabd->qk", flat, windows_three, preferred_element_type=jnp.float32)
    chan_in = windows_three.shape[0] // 8
    terms = terms.reshape(8, chan_out, 8, chan_in)
    lookup = jnp.asarray(tap_tables(), jnp.float32)
    return jnp.einsum("spk,posc->koc", lookup, terms, precision=HIGH)


def shards(coarse, w_three, w_four, elec_field, temp_grad, adjoint, adjoint_grad):
    groups_x = lax.axis_size("gx")
    chan_total, chan_in = (w_three.shape[1], w_three.shape[2])
    fine_x, fine_y, fine_z = adjoint.shape
    count_a, count_b = (fine_x // 4, fine_y // 4)
    cells = fine_x * groups_x * fine_y * lax.axis_size("gy") * fine_z
    rim_row = beside_y(coarse[:, :, :1], -1)
    ext_full = jnp.pad(jnp.concatenate([coarse, rim_row], 2), ((0, 0), (0, 1), (0, 0), (0, 0)))
    ext_brick = lax.dynamic_slice_in_dim(ext_full, lax.axis_index("gx") * count_a, count_a + 1, 1)
    windows_three = coarse_windows(ext_brick, count_a, count_b)
    pre_three = first_layer(windows_three, w_three)
    hidden = jax.nn.silu(pre_three).astype(jnp.bfloat16)
    hidden = hidden.reshape((2, 2, 2) + hidden.shape[1:])
    windows_four = hidden_windows(hidden)
    matrix_four = layer_four_matrix(w_four)
    out_four = jnp.einsum(
        "qk,kabd->qabd", matrix_four, windows_four, preferred_element_type=jnp.float32
    )
    density = to_storage(jax.nn.sigmoid(out_four), count_a, count_b)
    field_e = elec_field.astype(jnp.float32)
    energy = jnp.sum(field_e * field_e, axis=0)
    thermal = jnp.sum(temp_grad.astype(jnp.float32) * adjoint_grad.astype(jnp.float32), axis=0)
    adjoint_f = adjoint.astype(jnp.float32)
    sensitivity = (
        3.0 * (1.0 - 0.001) * density * density * energy * adjoint_f
        - 2.0 * (1.0 - 0.01) * density * thermal
    )
    scale = 8.0 / math.sqrt(cells)
    g_fine = (scale * sensitivity * density * (1.0 - density)).astype(jnp.bfloat16)
    g_classes = to_classes(g_fine, count_a, count_b)
    terms_four = jnp.einsum(
        "qabd,kabd->qk", g_classes, windows_four, preferred_element_type=jnp.float32
    )
    grad_four = jnp.einsum(
        "usk,usi->ki",
        jnp.asarray(residue_table(), jnp.float32),
        terms_four.reshape(64, 27, chan_total),
        precision=HIGH,
    )
    spread_back = jnp.einsum(
        "qk,qabd->kabd", matrix_four, g_classes, preferred_element_type=jnp.float32
    )
    spread_back = spread_back.reshape((3, 3, 3, chan_total) + spread_back.shape[1:])
    hidden_gradient = gather_back(spread_back).astype(jnp.bfloat16)
    g_pre = (hidden_gradient.astype(jnp.float32) * silu_slope(pre_three)).astype(jnp.bfloat16)
    grad_three = three_gradient(g_pre, windows_three)
    grad_three, grad_four = lax.psum((grad_three, grad_four), ("gx", "gy"))
    return (density, grad_three, grad_four)


def solution(mesh):
    return jax.shard_map(
        shards,
        mesh=mesh,
        in_specs=(
            P(None, None, "gy", None),
            P(),
            P(),
            P(None, "gx", "gy", None),
            P(None, "gx", "gy", None),
            P("gx", "gy", None),
            P(None, "gx", "gy", None),
        ),
        out_specs=(P("gx", "gy", None), P(), P()),
        check_vma=False,
    )
```

profile of v0, /device:TPU:0, one launch (start us, length us, event | category | flops | bytes accessed | tf_op | source)
XLA Modules:
  0.0 97.6 jit_solution(15323634922617167889)
XLA Ops:
  0.7 1.2 %slice.103 = bf16[32,8,1,128]{3,2,1,0:T(2,128)(2,1)S(1)} slice(bf16[32,8,16,128]{3,2,1,0:T(8,128)(2,1)} %param.11), slice={[0:32], [0:8], [0:1], [0:128]} | slice | bytes 131072 | tf_op jit(solution)/shard_map/slice | solution.py:168
  1.9 1.3 %collective-permute-start = (bf16[32,8,1,128]{3,2,1,0:T(2,128)(2,1)S(1)}, bf16[32,8,1,128]{3,2,1,0:T(2,128)(2,1)S(1)}, u32[]{:S(2)}, u32[]{:S(2)}) collective-permute-start(bf16[32,8,1,128]{3,2,1,0:T(2,128)(2,1)S(1)} %slice.103), channel_id=1, source_target_pairs={{1,0},{2,1},{3,2},{5,4},{6,5},{7,6},{9,8},{10,9},{11,10},{13,12},{... | collective-permute-start | bytes 196616 | tf_op jit(solution)/shard_map/ppermute | solution.py:14
  3.2 1.1 %fusion.6 = bf16[8,16,8,32]{3,0,1,2:T(8,128)(2,1)S(1)} fusion(bf16[8,8,27,1]{2,1,3,0:T(8,128)(2,1)} %constant.59, bf16[27,16,32]{2,1,0:T(8,128)(2,1)} %param.12), kind=kOutput, calls=%fused_computation.26 | convolution fusion | flops 1802240 | bytes 96640 | tf_op jit(solution)/shard_map/spk,koc->posc/dot_general | solution.py:90
  4.7 5.6 %collective-permute-done = bf16[32,8,1,128]{3,2,1,0:T(2,128)(2,1)S(1)} collective-permute-done((bf16[32,8,1,128]{3,2,1,0:T(2,128)(2,1)S(1)}, bf16[32,8,1,128]{3,2,1,0:T(2,128)(2,1)S(1)}, u32[]{:S(2)}, u32[]{:S(2)}) %collective-permute-start) | collective-permute-done | bytes 65568 | tf_op jit(solution)/shard_map/ppermute | solution.py:14
  12.3 1.4 %collective-permute-start.1 = (bf16[2,2,16,1,16,128]{5,2,4,1,0,3:T(8,128)(2,1)S(1)}, bf16[2,2,16,1,16,128]{5,2,4,1,0,3:T(8,128)(2,1)S(1)}, u32[]{:S(2)}, u32[]{:S(2)}) collective-permute-start(bf16[2,2,16,1,16,128]{5,2,4,1,0,3:T(8,128)(2,1)S(1)} %copy.49), channel_id=1, source_target_pairs={{4,0},{8,4},{12,8},{16,12},{20,16},{24,20},{28,24},{5,1},{9,5},{13... | collective-permute-start | bytes 786440 | tf_op jit(solution)/shard_map/ppermute | solution.py:14
  13.8 1.4 %multiply_reduce_fusion = (f32[4,64,512]{2,1,0:T(8,128)}, f32[4,64,512]{2,1,0:T(8,128)}) fusion(bf16[3,4,64,512]{3,2,1,0:T(8,128)(2,1)S(1)} %copy-done.4, bf16[3,4,64,512]{3,2,1,0:T(8,128)(2,1)S(1)} %copy-done.5, bf16[3,4,64,512]{3,2,1,0:T(8,128)(2,1)S(1)} %copy-done.6), kind=kLoop, calls=%fused_computation.11 | loop fusion | flops 2490368 | bytes 3407872 | tf_op jit(solution)/shard_map/reduce_sum | solution.py:183
  15.1 0.7 collective-permute-done.1
  16.0 1.3 %collective-permute-start.2 = (bf16[3,2,16,1,1,128]{5,2,0,4,1,3:T(8,128)(2,1)S(1)}, bf16[3,2,16,1,1,128]{5,2,0,4,1,3:T(8,128)(2,1)S(1)}, u32[]{:S(2)}, u32[]{:S(2)}) collective-permute-start(bf16[3,2,16,1,1,128]{5,2,0,4,1,3:T(8,128)(2,1)S(1)} %slice.145), channel_id=1, source_target_pairs={{1,0},{2,1},{3,2},{5,4},{6,5},{7,6},{9,8},{10,9},{11,10},{13,12},{... | collective-permute-start | bytes 73736 | tf_op jit(solution)/shard_map/ppermute | solution.py:14
  17.6 4.8 %collective-permute-done.2 = bf16[3,2,16,1,1,128]{5,2,0,4,1,3:T(8,128)(2,1)S(1)} collective-permute-done((bf16[3,2,16,1,1,128]{5,2,0,4,1,3:T(8,128)(2,1)S(1)}, bf16[3,2,16,1,1,128]{5,2,0,4,1,3:T(8,128)(2,1)S(1)}, u32[]{:S(2)}, u32[]{:S(2)}) %collective-permute-start.2) | collective-permute-done | bytes 24608 | tf_op jit(solution)/shard_map/ppermute | solution.py:14
  23.2 0.5 fusion.3
  23.8 1.0 %reshape.154 = f32[4,64,512]{2,1,0:T(8,128)} reshape(f32[1,4,16,4,4,128]{5,4,3,2,1,0:T(4,128)S(1)} %copy.55) | data formatting | bytes 1048576 | tf_op jit(solution)/shard_map/reshape | solution.py:135
  24.8 1.7 %fusion.23 = bf16[4,64,512]{2,1,0:T(8,128)(2,1)S(1)} fusion(f32[4,64,512]{2,1,0:T(8,128)} %reshape.154, f32[4,64,512]{2,1,0:T(8,128)} %get-tuple-element.20, f32[4,64,512]{2,1,0:T(8,128)} %get-tuple-element.19, bf16[4,64,512]{2,1,0:T(8,128)(2,1)} %param.16), kind=kLoop, calls=%fused_computation.52 | loop fusion | flops 1703936 | bytes 2097152 | tf_op jit(solution)/shard_map/convert_element_type | solution.py:190
  26.6 0.6 convolution_bitcast_fusion
  27.9 4.8 %collective-permute-start.3 = (f32[3,2,16,1,1,128]{5,2,4,1,0,3:T(8,128)S(1)}, f32[3,2,16,1,1,128]{5,2,4,1,0,3:T(8,128)S(1)}, u32[]{:S(2)}, u32[]{:S(2)}) collective-permute-start(f32[3,2,16,1,1,128]{5,2,4,1,0,3:T(8,128)S(1)} %slice.157), channel_id=1, source_target_pairs={{0,1},{1,2},{2,3},{4,5},{5,6},{6,7},{8,9},{9,10},{10,11},{12,13},{... | collective-permute-start | bytes 147464 | tf_op jit(solution)/shard_map/ppermute | solution.py:14
  32.8 1.7 %collective-permute-done.3 = f32[3,2,16,1,1,128]{5,2,4,1,0,3:T(8,128)S(1)} collective-permute-done((f32[3,2,16,1,1,128]{5,2,4,1,0,3:T(8,128)S(1)}, f32[3,2,16,1,1,128]{5,2,4,1,0,3:T(8,128)S(1)}, u32[]{:S(2)}, u32[]{:S(2)}) %collective-permute-start.3) | collective-permute-done | bytes 49184 | tf_op jit(solution)/shard_map/ppermute | solution.py:14
  34.7 4.3 %collective-permute-start.4 = (f32[2,2,16,1,16,128]{5,2,4,1,0,3:T(8,128)S(1)}, f32[2,2,16,1,16,128]{5,2,4,1,0,3:T(8,128)S(1)}, u32[]{:S(2)}, u32[]{:S(2)}) collective-permute-start(f32[2,2,16,1,16,128]{5,2,4,1,0,3:T(8,128)S(1)} %slice_bitcast_fusion.3), channel_id=1, source_target_pairs={{0,4},{4,8},{8,12},{12,16},{16,20},{20,24},{24,28},{1,5},{5,9},{9,... | collective-permute-start | bytes 1572872 | tf_op jit(solution)/shard_map/ppermute | solution.py:14
  39.0 0.6 fusion.41
  39.7 0.5 convolution_bitcast_fusion.2
  40.8 0.4 multiply_convert_fusion
  41.2 0.8 copy-done.3
  42.1 1.0 fusion.7
  43.0 0.6 convolution_bitcast_fusion.1
  43.6 53.2 %all-reduce.7 = (f32[27,16,32]{2,0,1:T(8,128)S(1)}, f32[27,16]{0,1:T(8,128)}) all-reduce(f32[27,16,32]{2,0,1:T(8,128)S(1)} %convolution_bitcast_fusion.1, f32[27,16]{0,1:T(8,128)S(1)} %convolution_bitcast_fusion.2), channel_id=1, replica_groups=mesh['gx'=8,'gy'=4] {'gx','gy'}, use_global_device_ids=true, to_apply=%region_2.3 | all-reduce | flops 14256 | bytes 114048 | tf_op jit(solution)/shard_map/psum | solution.py:208
  96.8 0.8 copy.64
  (64 shorter events, 5.3 us)
Async XLA Ops:
  0.6 16.7 %copy-start = (bf16[27,16]{0,1:T(8,128)(2,1)S(1)}, bf16[27,16]{0,1:T(8,128)(2,1)}, u32[]{:S(2)}) copy-start(bf16[27,16]{0,1:T(8,128)(2,1)} %param.13) | copy-start | bytes 2596
  0.6 9.6 %copy-start.1 = (bf16[32,8,16,128]{3,2,1,0:T(8,128)(2,1)S(1)}, bf16[32,8,16,128]{3,2,1,0:T(8,128)(2,1)}, u32[]{:S(2)}) copy-start(bf16[32,8,16,128]{3,2,1,0:T(8,128)(2,1)} %param.11) | copy-start | bytes 3145732
  1.9 8.4 %collective-permute-start = (bf16[32,8,1,128]{3,2,1,0:T(2,128)(2,1)S(1)}, bf16[32,8,1,128]{3,2,1,0:T(2,128)(2,1)S(1)}, u32[]{:S(2)}, u32[]{:S(2)}) collective-permute-start(bf16[32,8,1,128]{3,2,1,0:T(2,128)(2,1)S(1)} %slice.103), channel_id=1, source_target_pairs={{1,0},{2,1},{3,2},{5,4},{6,5},{7,6},{9,8},{10,9},{11,10},{13,12},{... | collective-permute-start | bytes 196616 | tf_op jit(solution)/shard_map/ppermute | solution.py:14
  11.0 1.0 copy-start.2
  11.9 1.8 %copy-start.4 = (bf16[3,4,64,512]{3,2,1,0:T(8,128)(2,1)S(1)}, bf16[3,4,64,512]{3,2,1,0:T(8,128)(2,1)}, u32[]{:S(2)}) copy-start(bf16[3,4,64,512]{3,2,1,0:T(8,128)(2,1)} %param.17) | copy-start | bytes 2359300
  11.9 1.8 %copy-start.5 = (bf16[3,4,64,512]{3,2,1,0:T(8,128)(2,1)S(1)}, bf16[3,4,64,512]{3,2,1,0:T(8,128)(2,1)}, u32[]{:S(2)}) copy-start(bf16[3,4,64,512]{3,2,1,0:T(8,128)(2,1)} %param.15) | copy-start | bytes 2359300
  11.9 1.8 %copy-start.6 = (bf16[3,4,64,512]{3,2,1,0:T(8,128)(2,1)S(1)}, bf16[3,4,64,512]{3,2,1,0:T(8,128)(2,1)}, u32[]{:S(2)}) copy-start(bf16[3,4,64,512]{3,2,1,0:T(8,128)(2,1)} %param.14) | copy-start | bytes 2359300
  12.3 3.6 %collective-permute-start.1 = (bf16[2,2,16,1,16,128]{5,2,4,1,0,3:T(8,128)(2,1)S(1)}, bf16[2,2,16,1,16,128]{5,2,4,1,0,3:T(8,128)(2,1)S(1)}, u32[]{:S(2)}, u32[]{:S(2)}) collective-permute-start(bf16[2,2,16,1,16,128]{5,2,4,1,0,3:T(8,128)(2,1)S(1)} %copy.49), channel_id=1, source_target_pairs={{4,0},{8,4},{12,8},{16,12},{20,16},{24,20},{28,24},{5,1},{9,5},{13... | collective-permute-start | bytes 786440 | tf_op jit(solution)/shard_map/ppermute | solution.py:14
  15.1 2.2 %copy-start.8 = (bf16[64,27,27]{0,2,1:T(8,128)(2,1)S(1)}, bf16[64,27,27]{0,2,1:T(8,128)(2,1)}, u32[]{:S(2)}) copy-start(bf16[64,27,27]{0,2,1:T(8,128)(2,1)} %constant.38.clone) | copy-start | bytes 279940
  16.0 6.3 %collective-permute-start.2 = (bf16[3,2,16,1,1,128]{5,2,0,4,1,3:T(8,128)(2,1)S(1)}, bf16[3,2,16,1,1,128]{5,2,0,4,1,3:T(8,128)(2,1)S(1)}, u32[]{:S(2)}, u32[]{:S(2)}) collective-permute-start(bf16[3,2,16,1,1,128]{5,2,0,4,1,3:T(8,128)(2,1)S(1)} %slice.145), channel_id=1, source_target_pairs={{1,0},{2,1},{3,2},{5,4},{6,5},{7,6},{9,8},{10,9},{11,10},{13,12},{... | collective-permute-start | bytes 73736 | tf_op jit(solution)/shard_map/ppermute | solution.py:14
  27.9 6.6 %collective-permute-start.3 = (f32[3,2,16,1,1,128]{5,2,4,1,0,3:T(8,128)S(1)}, f32[3,2,16,1,1,128]{5,2,4,1,0,3:T(8,128)S(1)}, u32[]{:S(2)}, u32[]{:S(2)}) collective-permute-start(f32[3,2,16,1,1,128]{5,2,4,1,0,3:T(8,128)S(1)} %slice.157), channel_id=1, source_target_pairs={{0,1},{1,2},{2,3},{4,5},{5,6},{6,7},{8,9},{9,10},{10,11},{12,13},{... | collective-permute-start | bytes 147464 | tf_op jit(solution)/shard_map/ppermute | solution.py:14
  34.7 5.0 %copy-start.7 = (f32[64,27,27]{0,2,1:T(8,128)S(1)}, f32[64,27,27]{0,2,1:T(8,128)}, u32[]{:S(2)}) copy-start(f32[64,27,27]{0,2,1:T(8,128)} %constant.39.clone) | copy-start | bytes 559876
  34.7 5.8 %collective-permute-start.4 = (f32[2,2,16,1,16,128]{5,2,4,1,0,3:T(8,128)S(1)}, f32[2,2,16,1,16,128]{5,2,4,1,0,3:T(8,128)S(1)}, u32[]{:S(2)}, u32[]{:S(2)}) collective-permute-start(f32[2,2,16,1,16,128]{5,2,4,1,0,3:T(8,128)S(1)} %slice_bitcast_fusion.3), channel_id=1, source_target_pairs={{0,4},{4,8},{8,12},{12,16},{16,20},{20,24},{24,28},{1,5},{5,9},{9,... | collective-permute-start | bytes 1572872 | tf_op jit(solution)/shard_map/ppermute | solution.py:14
  40.8 1.2 %copy-start.3 = (bf16[8,32,1,16,128]{4,3,1,2,0:T(8,128)(2,1)S(1)}, bf16[8,32,1,16,128]{4,3,1,2,0:T(8,128)(2,1)}, u32[]{:S(2)}) copy-start(bf16[8,32,1,16,128]{4,3,1,2,0:T(8,128)(2,1)} %copy-done.2) | copy-start | bytes 3145732
  42.1 1.0 copy-start.9
where the time goes:
time: 98 us; the launch traced here: 97.6 us
  blocking collectives  53.2 us (54%)
  starting transfers between devices  13.1 us (13%)
  waiting for transfers between devices  12.9 us (13%)
  local copies, waits for them, and re-layouts  6.6 us (7%)
  other arithmetic  5.36 us (5%)
  matrix products  5.33 us (5%)
  between operations  1.08 us (1%)
    psum x1, blocking collectives, shards(): grad_three, grad_four = lax.psum((grad_three, grad_four), ('gx', 'gy'))  53.2 us
    ppermute x5, starting transfers between devices, passed_along(): return lax.ppermute(value, axis, pairs)  13.1 us
    ppermute x5, waiting for transfers between devices, passed_along(): return lax.ppermute(value, axis, pairs)  12.9 us
    unnamed x28, local copies, waits for them, and re-layouts  2.32 us
  transfers between devices with their start and end apart: 5, of which 5 were waited for; matrix products, arithmetic and copies ran while one was open for 5% of the time, Pallas kernels for 0%

commit v1 on v0

--- a/solution.py
+++ b/solution.py
@@ -205,7 +205,7 @@
     hidden_gradient = gather_back(spread_back).astype(jnp.bfloat16)
     g_pre = (hidden_gradient.astype(jnp.float32) * silu_slope(pre_three)).astype(jnp.bfloat16)
     grad_three = three_gradient(g_pre, windows_three)
-    grad_three, grad_four = lax.psum((grad_three, grad_four), ("gx", "gy"))
+    grad_three, grad_four = lax.psum(lax.psum((grad_three, grad_four), "gy"), "gx")
     return (density, grad_three, grad_four)
 
 

time: 98 us -> 103 us (1.051)
  blocking collectives: 53.2 us -> 57.8 us
    psum x1 -> x2, blocking collectives: 53.2 us -> 57.8 us  [the longest x1 36.7 us: shards(): lax.psum(lax.psum((grad_three, grad_four), 'gy'), 'gx')]
  transfers between devices with their start and end apart: 5 -> 5, of which waited for: 5 -> 5; matrix products, arithmetic and copies ran while one was open for 5% -> 4% of each run, Pallas kernels for 0% -> 0%
where the time goes in v1:
time: 103 us; the launch traced here: 102 us
  blocking collectives  57.8 us (56%)
  starting transfers between devices  13.1 us (13%)
  waiting for transfers between devices  12.9 us (13%)
  local copies, waits for them, and re-layouts  6.59 us (6%)
  other arithmetic  5.39 us (5%)
  matrix products  5.33 us (5%)
  between operations  1.09 us (1%)
    psum x1, blocking collectives, shards(): lax.psum(lax.psum((grad_three, grad_four), 'gy'), 'gx')  36.7 us
    psum x1, blocking collectives, shards(): lax.psum((grad_three, grad_four), 'gy')  21.1 us
    ppermute x5, starting transfers between devices, passed_along(): return lax.ppermute(value, axis, pairs)  13.1 us
    ppermute x5, waiting for transfers between devices, passed_along(): return lax.ppermute(value, axis, pairs)  12.9 us
    unnamed x28, local copies, waits for them, and re-layouts  2.31 us
  transfers between devices with their start and end apart: 5, of which 5 were waited for; matrix products, arithmetic and copies ran while one was open for 4% of the time, Pallas kernels for 0%

profile of v1, /device:TPU:0, one launch (start us, length us, event | category | flops | bytes accessed | tf_op | source)
XLA Modules:
  0.0 102.2 jit_solution(6731726061736295494)
XLA Ops:
  0.7 1.2 %slice.103 = bf16[32,8,1,128]{3,2,1,0:T(2,128)(2,1)S(1)} slice(bf16[32,8,16,128]{3,2,1,0:T(8,128)(2,1)} %param.11), slice={[0:32], [0:8], [0:1], [0:128]} | slice | bytes 131072 | tf_op jit(solution)/shard_map/slice | solution.py:168
  1.9 1.3 %collective-permute-start = (bf16[32,8,1,128]{3,2,1,0:T(2,128)(2,1)S(1)}, bf16[32,8,1,128]{3,2,1,0:T(2,128)(2,1)S(1)}, u32[]{:S(2)}, u32[]{:S(2)}) collective-permute-start(bf16[32,8,1,128]{3,2,1,0:T(2,128)(2,1)S(1)} %slice.103), channel_id=1, source_target_pairs={{1,0},{2,1},{3,2},{5,4},{6,5},{7,6},{9,8},{10,9},{11,10},{13,12},{... | collective-permute-start | bytes 196616 | tf_op jit(solution)/shard_map/ppermute | solution.py:14
  3.2 1.1 %fusion.6 = bf16[8,16,8,32]{3,0,1,2:T(8,128)(2,1)S(1)} fusion(bf16[8,8,27,1]{2,1,3,0:T(8,128)(2,1)} %constant.59, bf16[27,16,32]{2,1,0:T(8,128)(2,1)} %param.12), kind=kOutput, calls=%fused_computation.26 | convolution fusion | flops 1802240 | bytes 96640 | tf_op jit(solution)/shard_map/spk,koc->posc/dot_general | solution.py:90
  4.7 5.6 %collective-permute-done = bf16[32,8,1,128]{3,2,1,0:T(2,128)(2,1)S(1)} collective-permute-done((bf16[32,8,1,128]{3,2,1,0:T(2,128)(2,1)S(1)}, bf16[32,8,1,128]{3,2,1,0:T(2,128)(2,1)S(1)}, u32[]{:S(2)}, u32[]{:S(2)}) %collective-permute-start) | collective-permute-done | bytes 65568 | tf_op jit(solution)/shard_map/ppermute | solution.py:14
  12.3 1.4 %collective-permute-start.1 = (bf16[2,2,16,1,16,128]{5,2,4,1,0,3:T(8,128)(2,1)S(1)}, bf16[2,2,16,1,16,128]{5,2,4,1,0,3:T(8,128)(2,1)S(1)}, u32[]{:S(2)}, u32[]{:S(2)}) collective-permute-start(bf16[2,2,16,1,16,128]{5,2,4,1,0,3:T(8,128)(2,1)S(1)} %copy.49), channel_id=1, source_target_pairs={{4,0},{8,4},{12,8},{16,12},{20,16},{24,20},{28,24},{5,1},{9,5},{13... | collective-permute-start | bytes 786440 | tf_op jit(solution)/shard_map/ppermute | solution.py:14
  13.7 1.4 %multiply_reduce_fusion = (f32[4,64,512]{2,1,0:T(8,128)}, f32[4,64,512]{2,1,0:T(8,128)}) fusion(bf16[3,4,64,512]{3,2,1,0:T(8,128)(2,1)S(1)} %copy-done.4, bf16[3,4,64,512]{3,2,1,0:T(8,128)(2,1)S(1)} %copy-done.5, bf16[3,4,64,512]{3,2,1,0:T(8,128)(2,1)S(1)} %copy-done.6), kind=kLoop, calls=%fused_computation.11 | loop fusion | flops 2490368 | bytes 3407872 | tf_op jit(solution)/shard_map/reduce_sum | solution.py:183
  15.1 0.7 collective-permute-done.1
  16.0 1.3 %collective-permute-start.2 = (bf16[3,2,16,1,1,128]{5,2,0,4,1,3:T(8,128)(2,1)S(1)}, bf16[3,2,16,1,1,128]{5,2,0,4,1,3:T(8,128)(2,1)S(1)}, u32[]{:S(2)}, u32[]{:S(2)}) collective-permute-start(bf16[3,2,16,1,1,128]{5,2,0,4,1,3:T(8,128)(2,1)S(1)} %slice.145), channel_id=1, source_target_pairs={{1,0},{2,1},{3,2},{5,4},{6,5},{7,6},{9,8},{10,9},{11,10},{13,12},{... | collective-permute-start | bytes 73736 | tf_op jit(solution)/shard_map/ppermute | solution.py:14
  17.6 4.8 %collective-permute-done.2 = bf16[3,2,16,1,1,128]{5,2,0,4,1,3:T(8,128)(2,1)S(1)} collective-permute-done((bf16[3,2,16,1,1,128]{5,2,0,4,1,3:T(8,128)(2,1)S(1)}, bf16[3,2,16,1,1,128]{5,2,0,4,1,3:T(8,128)(2,1)S(1)}, u32[]{:S(2)}, u32[]{:S(2)}) %collective-permute-start.2) | collective-permute-done | bytes 24608 | tf_op jit(solution)/shard_map/ppermute | solution.py:14
  23.2 0.5 fusion.3
  23.8 1.0 reshape.154
  24.8 1.7 %fusion.23 = bf16[4,64,512]{2,1,0:T(8,128)(2,1)S(1)} fusion(f32[4,64,512]{2,1,0:T(8,128)} %reshape.154, f32[4,64,512]{2,1,0:T(8,128)} %get-tuple-element.22, f32[4,64,512]{2,1,0:T(8,128)} %get-tuple-element.21, bf16[4,64,512]{2,1,0:T(8,128)(2,1)} %param.16), kind=kLoop, calls=%fused_computation.52 | loop fusion | flops 1703936 | bytes 2097152 | tf_op jit(solution)/shard_map/convert_element_type | solution.py:190
  26.6 0.6 convolution_bitcast_fusion
  27.9 4.8 %collective-permute-start.3 = (f32[3,2,16,1,1,128]{5,2,4,1,0,3:T(8,128)S(1)}, f32[3,2,16,1,1,128]{5,2,4,1,0,3:T(8,128)S(1)}, u32[]{:S(2)}, u32[]{:S(2)}) collective-permute-start(f32[3,2,16,1,1,128]{5,2,4,1,0,3:T(8,128)S(1)} %slice.157), channel_id=1, source_target_pairs={{0,1},{1,2},{2,3},{4,5},{5,6},{6,7},{8,9},{9,10},{10,11},{12,13},{... | collective-permute-start | bytes 147464 | tf_op jit(solution)/shard_map/ppermute | solution.py:14
  32.8 1.7 %collective-permute-done.3 = f32[3,2,16,1,1,128]{5,2,4,1,0,3:T(8,128)S(1)} collective-permute-done((f32[3,2,16,1,1,128]{5,2,4,1,0,3:T(8,128)S(1)}, f32[3,2,16,1,1,128]{5,2,4,1,0,3:T(8,128)S(1)}, u32[]{:S(2)}, u32[]{:S(2)}) %collective-permute-start.3) | collective-permute-done | bytes 49184 | tf_op jit(solution)/shard_map/ppermute | solution.py:14
  34.7 4.3 %collective-permute-start.4 = (f32[2,2,16,1,16,128]{5,2,4,1,0,3:T(8,128)S(1)}, f32[2,2,16,1,16,128]{5,2,4,1,0,3:T(8,128)S(1)}, u32[]{:S(2)}, u32[]{:S(2)}) collective-permute-start(f32[2,2,16,1,16,128]{5,2,4,1,0,3:T(8,128)S(1)} %slice_bitcast_fusion.3), channel_id=1, source_target_pairs={{0,4},{4,8},{8,12},{12,16},{16,20},{20,24},{24,28},{1,5},{5,9},{9,... | collective-permute-start | bytes 1572872 | tf_op jit(solution)/shard_map/ppermute | solution.py:14
  39.0 0.6 fusion.41
  39.7 0.5 convolution_bitcast_fusion.2
  41.2 0.8 copy-done.3
  42.1 1.0 fusion.7
  43.0 0.6 convolution_bitcast_fusion.1
  43.6 21.1 %all-reduce.8 = (f32[27,16,32]{2,0,1:T(8,128)S(1)}, f32[27,16]{0,1:T(8,128)S(1)}) all-reduce(f32[27,16,32]{2,0,1:T(8,128)S(1)} %convolution_bitcast_fusion.1, f32[27,16]{0,1:T(8,128)S(1)} %convolution_bitcast_fusion.2), channel_id=1, replica_groups=mesh['gx'=8,'gy'=4] {'gy'}, use_global_device_ids=true, to_apply=%region_2.3 | all-reduce | flops 14256 | bytes 114048 | tf_op jit(solution)/shard_map/psum | solution.py:208
  64.7 36.7 %all-reduce.7 = (f32[27,16,32]{2,0,1:T(8,128)S(1)}, f32[27,16]{0,1:T(8,128)}) all-reduce(f32[27,16,32]{2,0,1:T(8,128)S(1)} %get-tuple-element.11, f32[27,16]{0,1:T(8,128)S(1)} %get-tuple-element.12), channel_id=1, replica_groups=mesh['gx'=8,'gy'=4] {'gx'}, use_global_device_ids=true, to_apply=%region_3.4 | all-reduce | flops 14256 | bytes 114048 | tf_op jit(solution)/shard_map/psum | solution.py:208
  101.4 0.8 copy.64
  (65 shorter events, 5.7 us)
Async XLA Ops:
  0.6 16.7 %copy-start = (bf16[27,16]{0,1:T(8,128)(2,1)S(1)}, bf16[27,16]{0,1:T(8,128)(2,1)}, u32[]{:S(2)}) copy-start(bf16[27,16]{0,1:T(8,128)(2,1)} %param.13) | copy-start | bytes 2596
  0.6 9.6 %copy-start.1 = (bf16[32,8,16,128]{3,2,1,0:T(8,128)(2,1)S(1)}, bf16[32,8,16,128]{3,2,1,0:T(8,128)(2,1)}, u32[]{:S(2)}) copy-start(bf16[32,8,16,128]{3,2,1,0:T(8,128)(2,1)} %param.11) | copy-start | bytes 3145732
  1.9 8.4 %collective-permute-start = (bf16[32,8,1,128]{3,2,1,0:T(2,128)(2,1)S(1)}, bf16[32,8,1,128]{3,2,1,0:T(2,128)(2,1)S(1)}, u32[]{:S(2)}, u32[]{:S(2)}) collective-permute-start(bf16[32,8,1,128]{3,2,1,0:T(2,128)(2,1)S(1)} %slice.103), channel_id=1, source_target_pairs={{1,0},{2,1},{3,2},{5,4},{6,5},{7,6},{9,8},{10,9},{11,10},{13,12},{... | collective-permute-start | bytes 196616 | tf_op jit(solution)/shard_map/ppermute | solution.py:14
  11.0 1.0 copy-start.2
  11.9 1.8 %copy-start.4 = (bf16[3,4,64,512]{3,2,1,0:T(8,128)(2,1)S(1)}, bf16[3,4,64,512]{3,2,1,0:T(8,128)(2,1)}, u32[]{:S(2)}) copy-start(bf16[3,4,64,512]{3,2,1,0:T(8,128)(2,1)} %param.17) | copy-start | bytes 2359300
  11.9 1.8 %copy-start.5 = (bf16[3,4,64,512]{3,2,1,0:T(8,128)(2,1)S(1)}, bf16[3,4,64,512]{3,2,1,0:T(8,128)(2,1)}, u32[]{:S(2)}) copy-start(bf16[3,4,64,512]{3,2,1,0:T(8,128)(2,1)} %param.15) | copy-start | bytes 2359300
  11.9 1.8 %copy-start.6 = (bf16[3,4,64,512]{3,2,1,0:T(8,128)(2,1)S(1)}, bf16[3,4,64,512]{3,2,1,0:T(8,128)(2,1)}, u32[]{:S(2)}) copy-start(bf16[3,4,64,512]{3,2,1,0:T(8,128)(2,1)} %param.14) | copy-start | bytes 2359300
  12.3 3.6 %collective-permute-start.1 = (bf16[2,2,16,1,16,128]{5,2,4,1,0,3:T(8,128)(2,1)S(1)}, bf16[2,2,16,1,16,128]{5,2,4,1,0,3:T(8,128)(2,1)S(1)}, u32[]{:S(2)}, u32[]{:S(2)}) collective-permute-start(bf16[2,2,16,1,16,128]{5,2,4,1,0,3:T(8,128)(2,1)S(1)} %copy.49), channel_id=1, source_target_pairs={{4,0},{8,4},{12,8},{16,12},{20,16},{24,20},{28,24},{5,1},{9,5},{13... | collective-permute-start | bytes 786440 | tf_op jit(solution)/shard_map/ppermute | solution.py:14
  15.1 2.2 %copy-start.8 = (bf16[64,27,27]{0,2,1:T(8,128)(2,1)S(1)}, bf16[64,27,27]{0,2,1:T(8,128)(2,1)}, u32[]{:S(2)}) copy-start(bf16[64,27,27]{0,2,1:T(8,128)(2,1)} %constant.38.clone) | copy-start | bytes 279940
  16.0 6.3 %collective-permute-start.2 = (bf16[3,2,16,1,1,128]{5,2,0,4,1,3:T(8,128)(2,1)S(1)}, bf16[3,2,16,1,1,128]{5,2,0,4,1,3:T(8,128)(2,1)S(1)}, u32[]{:S(2)}, u32[]{:S(2)}) collective-permute-start(bf16[3,2,16,1,1,128]{5,2,0,4,1,3:T(8,128)(2,1)S(1)} %slice.145), channel_id=1, source_target_pairs={{1,0},{2,1},{3,2},{5,4},{6,5},{7,6},{9,8},{10,9},{11,10},{13,12},{... | collective-permute-start | bytes 73736 | tf_op jit(solution)/shard_map/ppermute | solution.py:14
  27.9 6.6 %collective-permute-start.3 = (f32[3,2,16,1,1,128]{5,2,4,1,0,3:T(8,128)S(1)}, f32[3,2,16,1,1,128]{5,2,4,1,0,3:T(8,128)S(1)}, u32[]{:S(2)}, u32[]{:S(2)}) collective-permute-start(f32[3,2,16,1,1,128]{5,2,4,1,0,3:T(8,128)S(1)} %slice.157), channel_id=1, source_target_pairs={{0,1},{1,2},{2,3},{4,5},{5,6},{6,7},{8,9},{9,10},{10,11},{12,13},{... | collective-permute-start | bytes 147464 | tf_op jit(solution)/shard_map/ppermute | solution.py:14
  34.7 5.0 %copy-start.7 = (f32[64,27,27]{0,2,1:T(8,128)S(1)}, f32[64,27,27]{0,2,1:T(8,128)}, u32[]{:S(2)}) copy-start(f32[64,27,27]{0,2,1:T(8,128)} %constant.39.clone) | copy-start | bytes 559876
  34.7 5.8 %collective-permute-start.4 = (f32[2,2,16,1,16,128]{5,2,4,1,0,3:T(8,128)S(1)}, f32[2,2,16,1,16,128]{5,2,4,1,0,3:T(8,128)S(1)}, u32[]{:S(2)}, u32[]{:S(2)}) collective-permute-start(f32[2,2,16,1,16,128]{5,2,4,1,0,3:T(8,128)S(1)} %slice_bitcast_fusion.3), channel_id=1, source_target_pairs={{0,4},{4,8},{8,12},{12,16},{16,20},{20,24},{24,28},{1,5},{5,9},{9,... | collective-permute-start | bytes 1572872 | tf_op jit(solution)/shard_map/ppermute | solution.py:14
  40.8 1.2 %copy-start.3 = (bf16[8,32,1,16,128]{4,3,1,2,0:T(8,128)(2,1)S(1)}, bf16[8,32,1,16,128]{4,3,1,2,0:T(8,128)(2,1)}, u32[]{:S(2)}) copy-start(bf16[8,32,1,16,128]{4,3,1,2,0:T(8,128)(2,1)} %copy-done.2) | copy-start | bytes 3145732
  42.1 1.0 copy-start.9
